TPU v7x, 32 devices: a whole 2x2x4 slice. The times are simulated.
32 devices in a mesh: grp: 4 (over y, x), tp: 8 (over z, core).
Axes of the slice: x: 2, y: 2, z: 4, core: 2. Of those that a mesh axis runs over, the one named last changes fastest.
Arguments:
- layer_input: bfloat16 [8192, 2048], P('grp'), may hold values from -6 to 6
- out_cotangent: bfloat16 [8192, 2048], P('grp'), may hold values from -6 to 6
- seq_group: int32 [6], replicated, may hold values from 0 to 3, as said below
- seq_len: int32 [6], replicated, may hold values from 512 to 2048, as said below
- w_qkv: float32 [2048, 6144], P('grp', 'tp'), may hold values from -0.1875 to 0.1875
- b_qv: float32 [4096], replicated, may hold values from -3 to 3
- w_out: float32 [2048, 2048], P('grp', 'tp'), may hold values from -0.75 to 0.75
- b_out: float32 [2048], replicated, may hold values from -2 to 2
- w_up: float32 [2048, 8192], P('grp', 'tp'), may hold values from -0.125 to 0.125
- b_up: float32 [8192], replicated, may hold values from -3 to 3
- w_down: float32 [2048, 8192], P('grp', 'tp'), may hold values from -0.0625 to 0.0625
- b_down: float32 [2048], replicated, may hold values from -2 to 2
- first_norm_gain: float32 [2048], replicated, may hold values from 0.1 to 1.9
- first_norm_bias: float32 [2048], replicated, may hold values from -2 to 2
- second_norm_gain: float32 [2048], replicated, may hold values from 0.1 to 1.9
- second_norm_bias: float32 [2048], replicated, may hold values from -2 to 2
Outputs:
- layer_output: bfloat16 [8192, 2048], P(('grp', 'tp'))
- grad_x: float32 [8192, 2048], P(('grp', 'tp'))
- grad_w_qkv: float32 [2048, 6144], P('grp', 'tp')
- grad_b_qv: float32 [4096], replicated
- grad_w_out: float32 [2048, 2048], P('grp', 'tp')
- grad_b_out: float32 [2048], replicated
- grad_w_up: float32 [2048, 8192], P('grp', 'tp')
- grad_b_up: float32 [8192], replicated
- grad_w_down: float32 [2048, 8192], P('grp', 'tp')
- grad_b_down: float32 [2048], replicated
- grad_ln1_gain: float32 [2048], replicated
- grad_ln1_bias: float32 [2048], replicated
- grad_ln2_gain: float32 [2048], replicated
- grad_ln2_bias: float32 [2048], replicated
Inputs may be any that keep to these rules, and one draw needn't show every extreme that they name: `seq_group`: each group's sequences total at most 2048 tokens, and in every draw some group holds exactly 2048; every group holds at least one sequence. `seq_len`: each sequence has 2048 or 512 tokens.
All inputs are finite; a program needn't handle non-finite values.
Results may differ from a plain program's by a relative error of at most 0.023.
Values may be sent and summed in bfloat16 or wider, within the bound.
A program may use at most 320 MiB of HBM per device.

v0:
```python
import jax
import jax.numpy as jnp
from jax import lax
from jax.sharding import PartitionSpec as P

HD = 128


def layer_normalize(rows, gain, bias):
    mean_row = jnp.mean(rows, -1, keepdims=True)
    centred = rows - mean_row
    inverse = lax.rsqrt(jnp.mean(centred * centred, -1, keepdims=True) + 1e-05)
    normed = centred * inverse
    return (normed * gain + bias, normed, inverse)


def norm_backward_pass(grad_norm, normed, inverse, gain):
    scaled = grad_norm * gain
    inner = jnp.mean(scaled, -1, keepdims=True) + normed * jnp.mean(
        scaled * normed, -1, keepdims=True
    )
    return inverse * (scaled - inner)


def contract(left, right, left_dim, right_dim):
    return lax.dot_general(
        left, right, (((left_dim,), (right_dim,)), ((), ())), preferred_element_type=jnp.float32
    )


def activate(values_in):
    return jax.nn.gelu(values_in, approximate=True)


def on_device(
    layer_input,
    out_cotangent,
    seq_group,
    seq_len,
    w_qkv,
    b_qv,
    w_out,
    b_out,
    w_up,
    b_up,
    w_down,
    b_down,
    first_norm_gain,
    first_norm_bias,
    second_norm_gain,
    second_norm_bias,
):
    w_attn, w_proj, w_expand, w_reduce = (
        lax.all_gather(w_qkv.astype(jnp.bfloat16), "grp", axis=0, tiled=True),
        lax.all_gather(w_out.astype(jnp.bfloat16), "grp", axis=0, tiled=True),
        lax.all_gather(w_up.astype(jnp.bfloat16), "grp", axis=0, tiled=True),
        lax.all_gather(w_down.astype(jnp.bfloat16), "grp", axis=0, tiled=True),
    )
    tp_rank = lax.axis_index("tp")
    tp_count = lax.axis_size("tp")
    group_rank = lax.axis_index("grp")
    length = layer_input.shape[0]
    shared_row_block = length // tp_count
    local_row_start = tp_rank * shared_row_block
    heads_here = w_proj.shape[1] // HD
    hidden_here = w_expand.shape[1]
    seq_count = seq_group.shape[0]
    in_group = seq_group == group_rank
    lengths = jnp.where(in_group, seq_len, 0)
    seq_order = jnp.arange(seq_count, dtype=jnp.int32)
    earlier = seq_order[:, None] > seq_order[None, :]
    offsets = jnp.sum(jnp.where(earlier, lengths[None, :], 0), 1)
    places = jnp.arange(length, dtype=jnp.int32)
    inside = (
        in_group[None, :]
        & (places[:, None] >= offsets[None, :])
        & (places[:, None] < (offsets + lengths)[None, :])
    )
    segment = jnp.sum(jnp.where(inside, seq_order[None, :] + 1, 0), 1) - 1
    live_rows = (segment >= 0).astype(jnp.float32)[:, None]
    input_row_block = layer_input.astype(jnp.float32)
    first_normalized, first_standardized, first_inverse_deviation = layer_normalize(
        input_row_block, first_norm_gain, first_norm_bias
    )
    normed_oneb = first_normalized.astype(jnp.bfloat16)
    head_bias = lax.dynamic_slice_in_dim(
        b_qv.reshape(-1, 2, HD), tp_rank * heads_here, heads_here, 0
    )
    bias_three = jnp.stack(
        [head_bias[:, 0], jnp.zeros_like(head_bias[:, 0]), head_bias[:, 1]], 1
    ).reshape(-1)
    projected = (
        jnp.dot(normed_oneb, w_attn, preferred_element_type=jnp.float32) + bias_three
    ).astype(jnp.bfloat16)
    projected = projected.reshape(length, heads_here, 3, HD)
    query = projected[:, :, 0]
    keys = projected[:, :, 1]
    values = projected[:, :, 2]
    block_rows = min(512, length)
    blocks = length // block_rows
    score_scale = HD ** (-0.5)
    columns = jnp.arange(length, dtype=jnp.int32)

    def scores_for(block_index):
        first_row = block_index * block_rows
        query_block = lax.dynamic_slice_in_dim(query, first_row, block_rows, 0)
        dotted = (
            jnp.einsum("qhe,khe->hqk", query_block, keys, preferred_element_type=jnp.float32)
            * score_scale
        )
        segment_block = lax.dynamic_slice_in_dim(segment, first_row, block_rows, 0)
        row_places = first_row + jnp.arange(block_rows, dtype=jnp.int32)
        allowed = (segment_block[:, None] == segment[None, :]) & (
            columns[None, :] <= row_places[:, None]
        )
        return (jnp.where(allowed[None], dotted, -1e30), query_block)

    def attend(block_index):
        masked, unused = scores_for(block_index)
        highest_score = jnp.max(masked, -1, keepdims=True)
        powers = jnp.exp(masked - highest_score)
        summed = jnp.sum(powers, -1, keepdims=True)
        chances = (powers / summed).astype(jnp.bfloat16)
        context = jnp.einsum(
            "hqk,khe->qhe", chances, values, preferred_element_type=jnp.float32
        ).astype(jnp.bfloat16)
        return (context, highest_score[..., 0] + jnp.log(summed[..., 0]))

    contexts, log_totals = lax.map(attend, jnp.arange(blocks))
    context_all = contexts.reshape(length, heads_here * HD)
    attn_total = lax.psum(contract(context_all, w_proj, 1, 1).astype(jnp.bfloat16), "tp").astype(
        jnp.float32
    )
    hidden_input = input_row_block + attn_total + b_out
    second_normalized, second_standardized, second_inverse_deviation = layer_normalize(
        hidden_input, second_norm_gain, second_norm_bias
    )
    normed_twob = second_normalized.astype(jnp.bfloat16)
    up_bias = lax.dynamic_slice_in_dim(b_up, tp_rank * hidden_here, hidden_here, 0)
    before = jnp.dot(normed_twob, w_expand, preferred_element_type=jnp.float32) + up_bias
    active = activate(before).astype(jnp.bfloat16)
    live_share = lax.dynamic_slice_in_dim(live_rows, local_row_start, shared_row_block, 0)
    mlp_total = lax.psum(contract(active, w_reduce, 1, 1).astype(jnp.bfloat16), "tp").astype(
        jnp.float32
    )
    out_share = (
        lax.dynamic_slice_in_dim(hidden_input, local_row_start, shared_row_block, 0)
        + lax.dynamic_slice_in_dim(mlp_total, local_row_start, shared_row_block, 0)
        + b_down
    )
    result = (live_share * out_share).astype(jnp.bfloat16)
    output_gradient = out_cotangent.astype(jnp.float32) * live_rows
    grad_outb = output_gradient.astype(jnp.bfloat16)
    grad_share = lax.dynamic_slice_in_dim(output_gradient, local_row_start, shared_row_block, 0)
    grad_reduce = contract(grad_outb, active, 0, 0)
    grad_active = jnp.dot(grad_outb, w_reduce, preferred_element_type=jnp.float32)
    unused, gelu_back = jax.vjp(activate, before)
    grad_beforeb = gelu_back(grad_active)[0].astype(jnp.bfloat16)
    grad_expand = contract(normed_twob, grad_beforeb, 0, 0)
    up_bias_part = jnp.sum(grad_beforeb.astype(jnp.float32), 0)
    second_norm_gradient = lax.psum(
        contract(grad_beforeb, w_expand, 1, 1).astype(jnp.bfloat16), "tp"
    ).astype(jnp.float32)
    hidden_gradient = output_gradient + norm_backward_pass(
        second_norm_gradient, second_standardized, second_inverse_deviation, second_norm_gain
    )
    grad_resb = hidden_gradient.astype(jnp.bfloat16)
    residual_share_gradient = lax.dynamic_slice_in_dim(
        hidden_gradient, local_row_start, shared_row_block, 0
    )
    second_norm_shared = lax.dynamic_slice_in_dim(
        second_norm_gradient, local_row_start, shared_row_block, 0
    )
    gain_two_grad = jnp.sum(
        second_norm_shared
        * lax.dynamic_slice_in_dim(second_standardized, local_row_start, shared_row_block, 0),
        0,
    )
    bias_two_grad = jnp.sum(second_norm_shared, 0)
    bias_out_grad = jnp.sum(residual_share_gradient, 0)
    down_bias_grad = jnp.sum(grad_share, 0)
    grad_proj = contract(grad_resb, context_all, 0, 0)
    grad_context = (
        jnp.dot(grad_resb, w_proj, preferred_element_type=jnp.float32)
        .astype(jnp.bfloat16)
        .reshape(length, heads_here, HD)
    )

    def attend_back(running, block_index):
        grad_keys, grad_values = running
        masked, query_block = scores_for(block_index)
        chances = jnp.exp(masked - log_totals[block_index][..., None])
        grad_block = lax.dynamic_slice_in_dim(grad_context, block_index * block_rows, block_rows, 0)
        grad_values = grad_values + jnp.einsum(
            "hqk,qhe->khe",
            chances.astype(jnp.bfloat16),
            grad_block,
            preferred_element_type=jnp.float32,
        )
        grad_chances = jnp.einsum(
            "qhe,khe->hqk", grad_block, values, preferred_element_type=jnp.float32
        )
        grad_scores = (
            chances * (grad_chances - jnp.sum(chances * grad_chances, -1, keepdims=True))
        ).astype(jnp.bfloat16)
        grad_query = (
            jnp.einsum("hqk,khe->qhe", grad_scores, keys, preferred_element_type=jnp.float32)
            * score_scale
        )
        grad_keys = (
            grad_keys
            + jnp.einsum(
                "hqk,qhe->khe", grad_scores, query_block, preferred_element_type=jnp.float32
            )
            * score_scale
        )
        return ((grad_keys, grad_values), grad_query)

    zeros_heads = jnp.zeros((length, heads_here, HD), jnp.float32)
    (grad_keys, grad_values), grad_queries = lax.scan(
        attend_back, (zeros_heads, zeros_heads), jnp.arange(blocks)
    )
    grad_queries = grad_queries.reshape(length, heads_here, HD)
    grad_projected = (
        jnp.stack([grad_queries, grad_keys, grad_values], 2)
        .astype(jnp.bfloat16)
        .reshape(length, heads_here * 3 * HD)
    )
    grad_attn = contract(normed_oneb, grad_projected, 0, 0)
    projected_sums = jnp.sum(grad_projected.astype(jnp.float32), 0).reshape(heads_here, 3, HD)
    query_value = jnp.stack([projected_sums[:, 0], projected_sums[:, 2]], 1)
    query_value_full = lax.dynamic_update_slice_in_dim(
        jnp.zeros((b_qv.shape[0] // (2 * HD), 2, HD), jnp.float32),
        query_value,
        tp_rank * heads_here,
        0,
    ).reshape(-1)
    up_bias_full = lax.dynamic_update_slice_in_dim(
        jnp.zeros(b_up.shape, jnp.float32), up_bias_part, tp_rank * hidden_here, 0
    )
    first_norm_gradient = lax.dynamic_slice_in_dim(
        lax.psum(contract(grad_projected, w_attn, 1, 1).astype(jnp.bfloat16), "tp").astype(
            jnp.float32
        ),
        local_row_start,
        shared_row_block,
        0,
    )
    shared_standardized = lax.dynamic_slice_in_dim(
        first_standardized, local_row_start, shared_row_block, 0
    )
    shared_inverse_deviation = lax.dynamic_slice_in_dim(
        first_inverse_deviation, local_row_start, shared_row_block, 0
    )
    input_gradient = residual_share_gradient + norm_backward_pass(
        first_norm_gradient, shared_standardized, shared_inverse_deviation, first_norm_gain
    )
    first_gain_gradient = jnp.sum(first_norm_gradient * shared_standardized, 0)
    bias_one_grad = jnp.sum(first_norm_gradient, 0)
    grads_attn, grads_proj, grads_expand, grads_reduce = (
        lax.psum_scatter(
            grad_attn.astype(jnp.bfloat16), "grp", scatter_dimension=0, tiled=True
        ).astype(jnp.float32),
        lax.psum_scatter(
            grad_proj.astype(jnp.bfloat16), "grp", scatter_dimension=0, tiled=True
        ).astype(jnp.float32),
        lax.psum_scatter(
            grad_expand.astype(jnp.bfloat16), "grp", scatter_dimension=0, tiled=True
        ).astype(jnp.float32),
        lax.psum_scatter(
            grad_reduce.astype(jnp.bfloat16), "grp", scatter_dimension=0, tiled=True
        ).astype(jnp.float32),
    )
    small_grads = lax.psum(
        (
            query_value_full,
            bias_out_grad,
            up_bias_full,
            down_bias_grad,
            first_gain_gradient,
            bias_one_grad,
            gain_two_grad,
            bias_two_grad,
        ),
        ("grp", "tp"),
    )
    return (
        result,
        input_gradient,
        grads_attn,
        small_grads[0],
        grads_proj,
        small_grads[1],
        grads_expand,
        small_grads[2],
        grads_reduce,
        small_grads[3],
        small_grads[4],
        small_grads[5],
        small_grads[6],
        small_grads[7],
    )


def solution(mesh):
    in_specs = (
        P("grp", None),
        P("grp", None),
        P(),
        P(),
        P("grp", "tp"),
        P(),
        P("grp", "tp"),
        P(),
        P("grp", "tp"),
        P(),
        P("grp", "tp"),
        P(),
        P(),
        P(),
        P(),
        P(),
    )
    out_specs = (
        P(("grp", "tp"), None),
        P(("grp", "tp"), None),
        P("grp", "tp"),
        P(),
        P("grp", "tp"),
        P(),
        P("grp", "tp"),
        P(),
        P("grp", "tp"),
        P(),
        P(),
        P(),
        P(),
        P(),
    )
    return jax.shard_map(
        on_device, mesh=mesh, in_specs=in_specs, out_specs=out_specs, check_vma=False
    )
```

profile of v0, /device:TPU:8, one launch (start us, length us, event | category | flops | bytes accessed | tf_op | source)
XLA Modules:
  0.0 1345.7 jit_solution(15598600205464487332)
XLA Ops:
  13.4 4.7 convert_reduce_fusion
  21.6 34.0 %all-gather.5.cloned.1.call-done = bf16[2048,768]{1,0:T(8,128)(2,1)} async-done(((bf16[512,768]{1,0:T(8,128)(2,1)}), bf16[2048,768]{1,0:T(8,128)(2,1)}) %all-gather.5.cloned.1.call-update) | async-done | bytes 3145744 | tf_op jit(solution)/shard_map/all_gather | solution.py:54
  55.6 11.5 add_convert_fusion.2
  71.4 46.1 %while.28 = (s32[]{:T(128)}, bf16[4,512,2,128]{3,2,1,0:T(2,128)(2,1)}, f32[4,2,512]{2,1,0:T(2,128)}, s32[4]{0:T(128)S(1)}, s32[2048]{0:T(1024)S(1)}, /*index=5*/...) while((s32[]{:T(128)}, ...), condition=%wide.region_7.8_spmd.clone, body=%wide.region_4.7_spmd.clone.sunk | while | flops 1102183936 | bytes 32557260 | solution.py:129
  117.5 8.2 convolution_convert_fusion.3
  132.2 169.3 %all-reduce.7.cloned.1.call-done = bf16[2048,2048]{1,0:T(8,128)(2,1)} async-done(((bf16[2048,2048]{1,0:T(8,128)(2,1)}), bf16[2048,2048]{1,0:T(8,128)(2,1)}) %all-reduce.7.cloned.1.call-update) | async-done | bytes 8388624 | tf_op jit(solution)/shard_map/psum | solution.py:131
  301.5 17.6 %fusion.88 = (f32[2048]{0:T(1024)S(1)}, f32[2048,2048]{1,0:T(8,128)}, f32[2048,2048]{1,0:T(8,128)}) fusion(f32[2048]{0:T(1024)S(1)} %copy-done.25, bf16[2048,2048]{1,0:T(8,128)(2,1)} %all-reduce.7.cloned.1.call-done, bf16[2048,2048]{1,0:T(8,128)(2,1)} %param.20, f32[2048]{0:T(1024)S(1)} %add_rsqrt_fusion.1, f32[2048]{0:T(1024)S(1)} %broadcast_multiply_fusion.3), kind=kLoop, calls=%fused_computation.141 | loop fusion | flops 29358080 | bytes 50364416 | tf_op jit(solution)/shard_map/reduce_sum | solution.py:10
  319.1 7.6 multiply_reduce_fusion.2
  326.7 11.8 subtract_multiply_fusion
  338.5 18.2 %all-gather.9.cloned.1.call-done = bf16[2048,1024]{1,0:T(8,128)(2,1)} async-done(((bf16[512,1024]{1,0:T(8,128)(2,1)}), bf16[2048,1024]{1,0:T(8,128)(2,1)}) %all-gather.9.cloned.1.call-update) | async-done | bytes 4194320 | tf_op jit(solution)/shard_map/all_gather | solution.py:56
  356.7 15.5 %fusion.75 = f32[2048,1024]{1,0:T(8,128)} fusion(bf16[2048,1024]{1,0:T(8,128)(2,1)} %all-gather.9.cloned.1.call-done, f32[2048,2048]{1,0:T(8,128)} %subtract_multiply_fusion, f32[2048]{0:T(1024)S(1)} %copy-done.31, f32[2048]{0:T(1024)S(1)} %copy-done.21), kind=kOutput, calls=%fused_computation.102 | convolution fusion | flops 8602517504 | bytes 29376512 | tf_op jit(solution)/shard_map/dot_general | solution.py:140
  372.2 39.5 %all-gather.11.cloned.1.call-done = bf16[2048,1024]{1,0:T(8,128)(2,1)} async-done(((bf16[512,1024]{1,0:T(8,128)(2,1)}), bf16[2048,1024]{1,0:T(8,128)(2,1)}) %all-gather.11.cloned.1.call-update) | async-done | bytes 4194320 | tf_op jit(solution)/shard_map/all_gather | solution.py:57
  411.7 19.5 %convert_reduce_fusion.1 = (f32[1024]{0:T(1024)}, bf16[2048,1024]{1,0:T(8,128)(2,1)S(1)}) fusion(f32[2048,1024]{1,0:T(8,128)} %fusion.75, f32[1024]{0:T(1024)S(1)} %dynamic_slice.59, bf16[2048,1024]{1,0:T(8,128)(2,1)} %all-gather.11.cloned.1.call-done, f32[2048]{0:T(1024)S(1)} %compare_convert_fusion, bf16[2048,2048]{1,0:T(8,128)(2,1)} %param.21), kind=kOutput, calls=%fused_computation.74 | convolution fusion | flops 8650750976 | bytes 25182208 | tf_op jit(solution)/shard_map/dot_general | solution.py:156
  433.2 10.9 convolution_convert_fusion.1
  444.1 175.7 %all-reduce.9.cloned.1.call-done = bf16[2048,2048]{1,0:T(8,128)(2,1)} async-done(((bf16[2048,2048]{1,0:T(8,128)(2,1)}), bf16[2048,2048]{1,0:T(8,128)(2,1)}) %all-reduce.9.cloned.1.call-update) | async-done | bytes 8388624 | tf_op jit(solution)/shard_map/psum | solution.py:161
  619.8 10.5 multiply_reduce_fusion.3
  630.3 19.1 %convert_multiply_fusion = (f32[2048,2048]{1,0:T(8,128)}, f32[2048,2048]{1,0:T(8,128)S(1)}) fusion(bf16[2048,2048]{1,0:T(8,128)(2,1)} %param.21, f32[2048]{0:T(1024)S(1)} %compare_convert_fusion, f32[2048]{0:T(1024)S(1)} %broadcast_multiply_fusion, f32[2048]{0:T(1024)S(1)} %broadcast_multiply_fusion.1, f32[2048]{0:T(1024)S(1)} %copy-done.21, ...), kind=kLoop, calls=%fused_computation.59 | loop fusion | flops 46137344 | bytes 67158016 | tf_op jit(solution)/shard_map/mul | solution.py:152
  649.4 5.7 copy-done
  658.8 16.8 %fusion.61 = bf16[2048,1024]{1,0:T(8,128)(2,1)} fusion(bf16[2048,2048]{1,0:T(8,128)(2,1)} %param.21, f32[2048]{0:T(1024)S(1)} %compare_convert_fusion, f32[2048,1024]{1,0:T(8,128)} %fusion.75, f32[1024]{0:T(1024)S(1)} %dynamic_slice.59), kind=kOutput, calls=%fused_computation.91 | convolution fusion | flops 8625586176 | bytes 20983808 | tf_op jit(solution)/shard_map/dot_general | solution.py:26
  675.7 15.3 %convolution_convert_fusion.4 = bf16[2048,1024]{1,0:T(8,128)(2,1)} fusion(bf16[2048,1024]{1,0:T(8,128)(2,1)} %copy-done.34, f32[2048,2048]{1,0:T(8,128)} %subtract_multiply_fusion, f32[2048]{0:T(1024)S(1)} %copy-done.31, f32[2048]{0:T(1024)S(1)} %copy-done.21), kind=kOutput, calls=%fused_computation.92 | convolution fusion | flops 8604614656 | bytes 25182208 | tf_op jit(solution)/shard_map/dot_general | solution.py:26
  691.1 9.8 fusion.67
  700.9 89.8 %while.29 = (s32[]{:T(128)}, f32[2048,2,128]{0,2,1:T(8,128)S(1)}, f32[2048,2,128]{0,2,1:T(8,128)}, bf16[4,512,2,128]{3,1,0,2:T(8,128)(2,1)}, s32[4]{0:T(128)S(1)...) while((s32[]{:T(128)}, f32[2048,2,128]{0,2,1:T(8,128)S(1)}, ...), condition=%wide.region_17.18_spmd.clone, body=%wide.region_15.17_spmd.clone.sunk | while | flops 2721709568 | bytes 97040784 | solution.py:220
  730.1 5.0 fusion.149
  752.8 5.0 fusion.149
  775.5 5.0 fusion.149
  800.1 13.1 convolution_convert_fusion.5
  813.2 17.8 %convolution_convert_fusion.2 = bf16[2048,2048]{1,0:T(8,128)(2,1)} fusion(bf16[2048,1024]{1,0:T(8,128)(2,1)} %all-gather.11.cloned.1.call-done, f32[2048,1024]{1,0:T(8,128)} %fusion.75, f32[1024]{0:T(1024)S(1)} %copy-done.28), kind=kOutput, calls=%fused_computation.78 | convolution fusion | flops 8615100416 | bytes 20975616 | tf_op jit(solution)/shard_map/dot_general | solution.py:26
  831.1 9.2 convolution_convert_fusion
  841.7 11.3 convert_element_type.149
  868.6 325.1 %all-reduce.13.cloned.1.call-done = (bf16[2048,2048]{1,0:T(8,128)(2,1)}, bf16[2048,2048]{1,0:T(8,128)(2,1)}) async-done(((bf16[2048,2048]{1,0:T(8,128)(2,1)}, bf16[2048,2048]{1,0:T(8,128)(2,1)}), (bf16[2048,2048]{1,0:T(8,128)(2,1)}, bf16[2048,2048]{1,0:T(8,128)(2,1)})) %all-reduce.13.cloned.1.call-update) | async-done | bytes 16777232 | tf_op jit(solution)/shard_map/psum | solution.py:143
  1196.9 5.2 dynamic-slice_reduce_fusion.2
  1205.3 122.7 %all-reduce.11.cloned.1.call-done = (f32[4096]{0:T(1024)}, f32[2048]{0:T(1024)}, f32[8192]{0:T(1024)}, f32[2048]{0:T(1024)}, f32[2048]{0:T(1024)}, /*index=5*/f32[2048]{0:T(1024)}, f32[2048]{0:T(1024)}, f32[2048]{0:T(1024)}) async-done(((f32[4096]{0:T(1024)}, f32[2048]{0:T(1024)}, f32[8192]{0:T(1024)}, f32[2048]{0:T(1024)}, f32[2048]{0:T(1024)}, /*index=5*/f32[2048]{0:T(1024)}, f32[2048]{0:T(1024)}, ...) | async-done | bytes 98320 | tf_op jit(solution)/shard_map/psum | solution.py:274
  (263 shorter events, 176.2 us)
Async XLA Ops:
  7.2 48.4 %all-gather.5.cloned.1.call-start = ((), (), s32[]{:S(2)}) async-start(), calls=%async_computation.4 | async-start | bytes 3932160 | tf_op jit(solution)/shard_map/all_gather | solution.py:54
  9.6 107.9 %all-gather.7.cloned.1.call-start = ((), (), s32[]{:S(2)}) async-start(), calls=%async_computation.5 | async-start | bytes 1310720 | tf_op jit(solution)/shard_map/all_gather | solution.py:55
  11.5 290.1 %all-reduce.7.cloned.1.call-start = ((), (), s32[]{:S(2)}) async-start(), calls=%async_computation.6 | async-start | bytes 16777216 | tf_op jit(solution)/shard_map/psum | solution.py:131
  13.4 42.2 %copy-start.22 = (f32[2048]{0:T(1024)S(1)}, f32[2048]{0:T(1024)}, u32[]{:S(2)}) copy-start(f32[2048]{0:T(1024)} %param.32) | copy-start | bytes 24580
  13.4 42.2 %copy-start.32 = (f32[2048]{0:T(1024)S(1)}, f32[2048]{0:T(1024)}, u32[]{:S(2)}) copy-start(f32[2048]{0:T(1024)} %param.33) | copy-start | bytes 24580
  19.2 282.3 %copy-start.15 = (f32[2048]{0:T(1024)}, f32[2048]{0:T(1024)S(1)}, u32[]{:S(2)}) copy-start(f32[2048]{0:T(1024)S(1)} %broadcast_multiply_fusion.3) | copy-start | bytes 24580
  21.6 280.0 %copy-start.19 = (f32[2048]{0:T(1024)}, f32[2048]{0:T(1024)S(1)}, u32[]{:S(2)}) copy-start(f32[2048]{0:T(1024)S(1)} %add_rsqrt_fusion.1) | copy-start | bytes 24580
  117.5 8.3 copy-start.1
  125.8 175.8 %copy-start.25 = (f32[2048]{0:T(1024)S(1)}, f32[2048]{0:T(1024)}, u32[]{:S(2)}) copy-start(f32[2048]{0:T(1024)} %param.27) | copy-start | bytes 24580
  125.8 230.8 %all-gather.9.cloned.1.call-start = ((), (), s32[]{:S(2)}) async-start(), calls=%async_computation.7 | async-start | bytes 5242880 | tf_op jit(solution)/shard_map/all_gather | solution.py:56
  128.6 283.0 %all-gather.11.cloned.1.call-start = ((), (), s32[]{:S(2)}) async-start(), calls=%async_computation.8 | async-start | bytes 5242880 | tf_op jit(solution)/shard_map/all_gather | solution.py:57
  131.4 488.4 %all-reduce.9.cloned.1.call-start = ((), (), s32[]{:S(2)}) async-start(), calls=%async_computation.9 | async-start | bytes 16777216 | tf_op jit(solution)/shard_map/psum | solution.py:161
  131.5 527.3 %copy-start.18 = (f32[2048]{0:T(1024)}, f32[2048]{0:T(1024)S(1)}, u32[]{:S(2)}) copy-start(f32[2048]{0:T(1024)S(1)} %compare_convert_fusion) | copy-start | bytes 24580
  132.2 526.6 %copy-start.27 = (f32[1024]{0:T(1024)}, f32[1024]{0:T(1024)S(1)}, u32[]{:S(2)}) copy-start(f32[1024]{0:T(1024)S(1)} %dynamic_slice.59) | copy-start | bytes 12292
  326.7 30.0 %copy-start.21 = (f32[2048]{0:T(1024)S(1)}, f32[2048]{0:T(1024)}, u32[]{:S(2)}) copy-start(f32[2048]{0:T(1024)} %param.34) | copy-start | bytes 24580
  326.7 30.0 %copy-start.31 = (f32[2048]{0:T(1024)S(1)}, f32[2048]{0:T(1024)}, u32[]{:S(2)}) copy-start(f32[2048]{0:T(1024)} %param.35) | copy-start | bytes 24580
  411.7 21.5 %copy-start.29 = (bf16[2048,1024]{1,0:T(8,128)(2,1)S(1)}, bf16[2048,1024]{1,0:T(8,128)(2,1)}, u32[]{:S(2)}) copy-start(bf16[2048,1024]{1,0:T(8,128)(2,1)} %all-gather.9.cloned.1.call-done) | copy-start | bytes 12582916
  444.1 414.6 %reduce-scatter.7.cloned.1.call-start = ((), (), s32[]{:S(2)}) async-start(), calls=%async_computation.11 | async-start | bytes 1310720 | tf_op jit(solution)/shard_map/reduce_scatter | solution.py:264
  630.3 24.8 %copy-start.8 = (bf16[4,512,2,128]{3,2,1,0:T(2,128)(2,1)S(1)}, bf16[4,512,2,128]{3,2,1,0:T(2,128)(2,1)}, u32[]{:S(2)}) copy-start(bf16[4,512,2,128]{3,2,1,0:T(2,128)(2,1)} %get-tuple-element.126) | copy-start | bytes 3145732
  658.7 201.7 %reduce-scatter.11.cloned.1.call-start = ((), (), s32[]{:S(2)}) async-start(), calls=%async_computation.13 | async-start | bytes 5242880 | tf_op jit(solution)/shard_map/reduce_scatter | solution.py:270
  675.7 187.6 %reduce-scatter.9.cloned.1.call-start = ((), (), s32[]{:S(2)}) async-start(), calls=%async_computation.12 | async-start | bytes 5242880 | tf_op jit(solution)/shard_map/reduce_scatter | solution.py:267
  691.1 9.8 copy-start.2
  691.1 9.8 copy-start.11
  691.1 174.9 %reduce-scatter.5.cloned.1.call-start = ((), (), s32[]{:S(2)}) async-start(), calls=%async_computation.10 | async-start | bytes 3932160 | tf_op jit(solution)/shard_map/reduce_scatter | solution.py:261
  800.1 13.2 copy-start.28
  813.2 17.9 %copy-start.9 = (bf16[2048,2,3,128]{0,3,2,1:T(8,128)(2,1)S(1)}, bf16[2048,2,3,128]{0,3,2,1:T(8,128)(2,1)}, u32[]{:S(2)}) copy-start(bf16[2048,2,3,128]{0,3,2,1:T(8,128)(2,1)} %copy.80) | copy-start | bytes 9437188
  813.2 380.5 %all-reduce.13.cloned.1.call-start = ((), (), s32[]{:S(2)}) async-start(), calls=%async_computation.15 | async-start | bytes 33554432 | tf_op jit(solution)/shard_map/psum | solution.py:143
  813.2 17.8 %copy-start.30 = (bf16[2048,768]{1,0:T(8,128)(2,1)S(1)}, bf16[2048,768]{1,0:T(8,128)(2,1)}, u32[]{:S(2)}) copy-start(bf16[2048,768]{1,0:T(8,128)(2,1)} %all-gather.5.cloned.1.call-done) | copy-start | bytes 9437188
  840.2 487.7 %all-reduce.11.cloned.1.call-start = ((), (), s32[]{:S(2)}) async-start(), calls=%async_computation.14 | async-start | bytes 196608 | tf_op jit(solution)/shard_map/psum | solution.py:274
  841.7 11.3 copy-start.14
  858.6 343.5 %copy-start.17 = (f32[16,2,128]{2,1,0:T(2,128)}, f32[16,2,128]{2,1,0:T(2,128)S(1)}, u32[]{:S(2)}) copy-start(f32[16,2,128]{2,1,0:T(2,128)S(1)} %constant_dynamic-update-slice_fusion) | copy-start | bytes 49156
  863.2 338.9 %copy-start.24 = (f32[2048]{0:T(1024)S(1)}, f32[2048]{0:T(1024)}, u32[]{:S(2)}) copy-start(f32[2048]{0:T(1024)} %param.31) | copy-start | bytes 24580
  (27 other events, 127.3 us)
Sparse Core Ops, SparseCore 0:
  10.4 45.1 all-gather.4
  58.0 26.6 all-gather.6
  125.9 175.5 all-reduce.6
  303.8 52.8 all-gather.8
  358.9 52.6 all-gather.10
  444.2 175.5 all-reduce.8
  658.8 27.8 reduce-scatter.6
  690.0 52.6 reduce-scatter.10
  745.7 52.6 reduce-scatter.8
  813.3 43.9 reduce-scatter.4
  860.1 333.5 all-reduce.12
  1202.2 125.6 all-reduce.10
where the time goes:
time: 1350 us
  waiting for transfers between devices  885 us (66%)
  matrix products  229 us (17%)
  other arithmetic  157 us (12%)
  local copies, waits for them, and re-layouts  45.9 us (3%)
  between operations  15.2 us (1%)
  loops' own time  14 us (1%)
    psum x1, waiting for transfers between devices, on_device(): lax.psum(contract(active, w_reduce, 1, 1).astype(jnp.bfloat16), 'tp')  325 us
    psum x1, waiting for transfers between devices, on_device(): lax.psum(contract(grad_beforeb, w_expand, 1, 1).astype(jnp.bfloat16), 'tp')  176 us
    psum x1, waiting for transfers between devices, on_device(): lax.psum(contract(context_all, w_proj, 1, 1).astype(jnp.bfloat16), 'tp')  169 us
    psum x1, waiting for transfers between devices, on_device(): lax.psum((query_value_full, bias_out_grad, up_bias_full, down_bias_grad,...  123 us
    dot_general x8, matrix products, contract(): lax.dot_general(left, right, (((left_dim,), (right_dim,)), ((), ())), pre...  94.9 us
    all_gather x1, waiting for transfers between devices, on_device(): lax.all_gather(w_down.astype(jnp.bfloat16), 'grp', axis=0, tiled=True)  39.5 us
    all_gather x1, waiting for transfers between devices, on_device(): lax.all_gather(w_qkv.astype(jnp.bfloat16), 'grp', axis=0, tiled=True)  34 us
  transfers between devices with their start and end apart: 12, of which 7 were waited for; matrix products, arithmetic and copies ran while one was open for 24% of the time, Pallas kernels for 0%

commit v1 on v0

--- a/solution.py
+++ b/solution.py
@@ -4,6 +4,27 @@
 from jax.sharding import PartitionSpec as P
 
 HD = 128
+
+
+def gather_around(x, axis, dim):
+    devices, position, rows = (lax.axis_size(axis), lax.axis_index(axis), x.shape[dim])
+    upward = [(i, (i + 1) % devices) for i in range(devices)]
+    left = [(i, (i - 1) % devices) for i in range(devices)]
+    out = jnp.zeros((*x.shape[:dim], devices * rows, *x.shape[dim + 1 :]), x.dtype)
+    out = lax.dynamic_update_slice_in_dim(out, x, position * rows, axis=dim)
+    from_left = from_right = x
+    halfway = devices // 2
+    for step in range(1, halfway + 1):
+        from_left = lax.ppermute(from_left, axis, upward)
+        out = lax.dynamic_update_slice_in_dim(
+            out, from_left, (position - step) % devices * rows, axis=dim
+        )
+        if step < devices - halfway:
+            from_right = lax.ppermute(from_right, axis, left)
+            out = lax.dynamic_update_slice_in_dim(
+                out, from_right, (position + step) % devices * rows, axis=dim
+            )
+    return out
 
 
 def layer_normalize(rows, gain, bias):
@@ -54,7 +75,7 @@
         lax.all_gather(w_qkv.astype(jnp.bfloat16), "grp", axis=0, tiled=True),
         lax.all_gather(w_out.astype(jnp.bfloat16), "grp", axis=0, tiled=True),
         lax.all_gather(w_up.astype(jnp.bfloat16), "grp", axis=0, tiled=True),
-        lax.all_gather(w_down.astype(jnp.bfloat16), "grp", axis=0, tiled=True),
+        gather_around(w_down.astype(jnp.bfloat16), "grp", 0),
     )
     tp_rank = lax.axis_index("tp")
     tp_count = lax.axis_size("tp")

time: 1350 us -> 1310 us (0.970)
  waiting for transfers between devices: 885 us -> 836 us
    psum x1, waiting for transfers between devices: 169 us -> 98.4 us  [on_device(): lax.psum(contract(context_all, w_proj, 1, 1).astype(jnp.bfloat16), 'tp')]
    ppermute x0 -> x3, waiting for transfers between devices: none -> 62 us  [the longest x2 43.2 us: gather_around(): from_left = lax.ppermute(from_left, axis, upward)]
    all_gather x1 -> x0, waiting for transfers between devices: 39.5 us -> none  [on_device(): lax.all_gather(w_down.astype(jnp.bfloat16), 'grp', axis=0, tiled=True)]
  transfers between devices with their start and end apart: 12 -> 14, of which waited for: 7 -> 9; matrix products, arithmetic and copies ran while one was open for 24% -> 24% of each run, Pallas kernels for 0% -> 0%
where the time goes in v1:
time: 1310 us
  waiting for transfers between devices  836 us (64%)
  matrix products  228 us (17%)
  other arithmetic  156 us (12%)
  local copies, waits for them, and re-layouts  52.8 us (4%)
  between operations  14.9 us (1%)
  loops' own time  14 us (1%)
    psum x1, waiting for transfers between devices, on_device(): lax.psum(contract(active, w_reduce, 1, 1).astype(jnp.bfloat16), 'tp')  325 us
    psum x1, waiting for transfers between devices, on_device(): lax.psum(contract(grad_beforeb, w_expand, 1, 1).astype(jnp.bfloat16), 'tp')  176 us
    psum x1, waiting for transfers between devices, on_device(): lax.psum((query_value_full, bias_out_grad, up_bias_full, down_bias_grad,...  123 us
    psum x1, waiting for transfers between devices, on_device(): lax.psum(contract(context_all, w_proj, 1, 1).astype(jnp.bfloat16), 'tp')  98.4 us
    dot_general x8, matrix products, contract(): lax.dot_general(left, right, (((left_dim,), (right_dim,)), ((), ())), pre...  94.9 us
    ppermute x2, waiting for transfers between devices, gather_around(): from_left = lax.ppermute(from_left, axis, upward)  43.2 us
    all_gather x1, waiting for transfers between devices, on_device(): lax.all_gather(w_qkv.astype(jnp.bfloat16), 'grp', axis=0, tiled=True)  34 us
  transfers between devices with their start and end apart: 14, of which 9 were waited for; matrix products, arithmetic and copies ran while one was open for 24% of the time, Pallas kernels for 0%

profile of v1, /device:TPU:8, one launch (start us, length us, event | category | flops | bytes accessed | tf_op | source)
XLA Modules:
  0.0 1305.5 jit_solution(8149133300228723358)
XLA Ops:
  21.6 34.0 %all-gather.4.cloned.1.call-done = bf16[2048,768]{1,0:T(8,128)(2,1)} async-done(((bf16[512,768]{1,0:T(8,128)(2,1)}), bf16[2048,768]{1,0:T(8,128)(2,1)}) %all-gather.4.cloned.1.call-update) | async-done | bytes 3145744 | tf_op jit(solution)/shard_map/all_gather | solution.py:75
  55.6 11.5 add_convert_fusion.2
  71.4 46.1 %while.28 = (s32[]{:T(128)}, bf16[4,512,2,128]{3,2,1,0:T(2,128)(2,1)}, f32[4,2,512]{2,1,0:T(2,128)}, s32[4]{0:T(128)S(1)}, s32[2048]{0:T(1024)S(1)}, /*index=5*/...) while((s32[]{:T(128)}, ...), condition=%wide.region_7.8_spmd.clone, body=%wide.region_4.7_spmd.clone.sunk | while | flops 1102183936 | bytes 32557260 | solution.py:150
  117.5 8.2 convolution_convert_fusion.3
  135.6 22.9 %collective-permute-done = bf16[512,1024]{1,0:T(8,128)(2,1)} collective-permute-done((bf16[512,1024]{1,0:T(8,128)(2,1)S(1)}, bf16[512,1024]{1,0:T(8,128)(2,1)}, u32[]{:S(2)}, u32[]{:S(2)}) %collective-permute-start) | collective-permute-done | bytes 1048608 | tf_op jit(solution)/shard_map/ppermute | solution.py:18
  161.9 18.8 %collective-permute-done.1 = bf16[512,1024]{1,0:T(8,128)(2,1)S(1)} collective-permute-done((bf16[512,1024]{1,0:T(8,128)(2,1)S(1)}, bf16[512,1024]{1,0:T(8,128)(2,1)S(1)}, u32[]{:S(2)}, u32[]{:S(2)}) %collective-permute-start.1) | collective-permute-done | bytes 1048608 | tf_op jit(solution)/shard_map/ppermute | solution.py:23
  181.7 20.4 %collective-permute-done.2 = bf16[512,1024]{1,0:T(8,128)(2,1)S(1)} collective-permute-done((bf16[512,1024]{1,0:T(8,128)(2,1)}, bf16[512,1024]{1,0:T(8,128)(2,1)S(1)}, u32[]{:S(2)}, u32[]{:S(2)}) %collective-permute-start.2) | collective-permute-done | bytes 1048608 | tf_op jit(solution)/shard_map/ppermute | solution.py:18
  203.2 98.4 %all-reduce.7.cloned.1.call-done = bf16[2048,2048]{1,0:T(8,128)(2,1)} async-done(((bf16[2048,2048]{1,0:T(8,128)(2,1)}), bf16[2048,2048]{1,0:T(8,128)(2,1)}) %all-reduce.7.cloned.1.call-update) | async-done | bytes 8388624 | tf_op jit(solution)/shard_map/psum | solution.py:152
  301.5 17.6 %fusion.88 = (f32[2048]{0:T(1024)S(1)}, f32[2048,2048]{1,0:T(8,128)}, f32[2048,2048]{1,0:T(8,128)}) fusion(f32[2048]{0:T(1024)S(1)} %copy-done.26, bf16[2048,2048]{1,0:T(8,128)(2,1)} %all-reduce.7.cloned.1.call-done, bf16[2048,2048]{1,0:T(8,128)(2,1)} %param.20, f32[2048]{0:T(1024)S(1)} %add_rsqrt_fusion.1, f32[2048]{0:T(1024)S(1)} %broadcast_multiply_fusion.3), kind=kLoop, calls=%fused_computation.145 | loop fusion | flops 29358080 | bytes 50364416 | tf_op jit(solution)/shard_map/reduce_sum | solution.py:31
  319.1 7.6 multiply_reduce_fusion.2
  326.7 11.8 subtract_multiply_fusion
  338.5 18.1 %all-gather.8.cloned.1.call-done = bf16[2048,1024]{1,0:T(8,128)(2,1)} async-done(((bf16[512,1024]{1,0:T(8,128)(2,1)}), bf16[2048,1024]{1,0:T(8,128)(2,1)}) %all-gather.8.cloned.1.call-update) | async-done | bytes 4194320 | tf_op jit(solution)/shard_map/all_gather | solution.py:77
  356.7 13.2 %fusion.75 = f32[2048,1024]{1,0:T(8,128)S(1)} fusion(bf16[2048,1024]{1,0:T(8,128)(2,1)} %all-gather.8.cloned.1.call-done, f32[2048,2048]{1,0:T(8,128)} %subtract_multiply_fusion, f32[2048]{0:T(1024)S(1)} %copy-done.32, f32[2048]{0:T(1024)S(1)} %copy-done.22), kind=kOutput, calls=%fused_computation.102 | convolution fusion | flops 8602517504 | bytes 29376512 | tf_op jit(solution)/shard_map/dot_general | solution.py:161
  369.9 21.4 %convert_reduce_fusion.1 = (f32[1024]{0:T(1024)}, bf16[2048,1024]{1,0:T(8,128)(2,1)S(1)}) fusion(f32[2048,1024]{1,0:T(8,128)S(1)} %fusion.75, f32[1024]{0:T(1024)S(1)} %dynamic_slice.59, bf16[2048,1024]{1,0:T(8,128)(2,1)} %constant_dynamic-update-slice_fusion.1, f32[2048]{0:T(1024)S(1)} %compare_convert_fusion, bf16[2048,2048]{1,0:T(8,128)(2,1)} %param.21), kind=kOutput, calls=%fused_computation.74 | convolution fusion | flops 8650750976 | bytes 25182208 | tf_op jit(solution)/shard_map/dot_general | solution.py:177
  393.2 10.9 convolution_convert_fusion.1
  404.2 175.7 %all-reduce.9.cloned.1.call-done = bf16[2048,2048]{1,0:T(8,128)(2,1)} async-done(((bf16[2048,2048]{1,0:T(8,128)(2,1)}), bf16[2048,2048]{1,0:T(8,128)(2,1)}) %all-reduce.9.cloned.1.call-update) | async-done | bytes 8388624 | tf_op jit(solution)/shard_map/psum | solution.py:182
  579.9 10.5 multiply_reduce_fusion.3
  590.4 19.1 %convert_multiply_fusion = (f32[2048,2048]{1,0:T(8,128)}, f32[2048,2048]{1,0:T(8,128)S(1)}) fusion(bf16[2048,2048]{1,0:T(8,128)(2,1)} %param.21, f32[2048]{0:T(1024)S(1)} %compare_convert_fusion, f32[2048]{0:T(1024)S(1)} %broadcast_multiply_fusion, f32[2048]{0:T(1024)S(1)} %broadcast_multiply_fusion.1, f32[2048]{0:T(1024)S(1)} %copy-done.22, ...), kind=kLoop, calls=%fused_computation.59 | loop fusion | flops 46137344 | bytes 67158016 | tf_op jit(solution)/shard_map/mul | solution.py:173
  609.5 5.7 copy-done
  618.9 16.8 %fusion.61 = bf16[2048,1024]{1,0:T(8,128)(2,1)} fusion(bf16[2048,2048]{1,0:T(8,128)(2,1)} %param.21, f32[2048]{0:T(1024)S(1)} %compare_convert_fusion, f32[2048,1024]{1,0:T(8,128)} %copy-done.35, f32[1024]{0:T(1024)S(1)} %dynamic_slice.59), kind=kOutput, calls=%fused_computation.91 | convolution fusion | flops 8625586176 | bytes 20983808 | tf_op jit(solution)/shard_map/dot_general | solution.py:47
  635.9 15.3 %convolution_convert_fusion.4 = bf16[2048,1024]{1,0:T(8,128)(2,1)} fusion(bf16[2048,1024]{1,0:T(8,128)(2,1)} %copy-done.36, f32[2048,2048]{1,0:T(8,128)} %subtract_multiply_fusion, f32[2048]{0:T(1024)S(1)} %copy-done.32, f32[2048]{0:T(1024)S(1)} %copy-done.22), kind=kOutput, calls=%fused_computation.92 | convolution fusion | flops 8604614656 | bytes 25182208 | tf_op jit(solution)/shard_map/dot_general | solution.py:47
  651.3 9.8 fusion.67
  661.0 89.8 %while.29 = (s32[]{:T(128)}, f32[2048,2,128]{0,2,1:T(8,128)S(1)}, f32[2048,2,128]{0,2,1:T(8,128)}, bf16[4,512,2,128]{3,1,0,2:T(8,128)(2,1)}, s32[4]{0:T(128)S(1)...) while((s32[]{:T(128)}, f32[2048,2,128]{0,2,1:T(8,128)S(1)}, ...), condition=%wide.region_17.18_spmd.clone, body=%wide.region_15.17_spmd.clone.sunk | while | flops 2721709568 | bytes 97040784 | solution.py:241
  690.2 5.0 fusion.149
  712.9 5.0 fusion.149
  760.2 13.1 %convolution_convert_fusion.5 = bf16[2048,768]{1,0:T(8,128)(2,1)} fusion(bf16[2048,768]{0,1:T(8,128)(2,1)} %bitcast.102, f32[2048]{0:T(1024)S(1)} %copy-done.34, f32[2048]{0:T(1024)S(1)} %copy-done.24, bf16[2048,2048]{1,0:T(8,128)(2,1)} %param.20, f32[2048]{0:T(1024)S(1)} %copy-done.21, f32[2048]{0:T(1024)S(1)} %copy-done.17), kind=kOutput, calls=%fused_computation.93 | convolution fusion | flops 6469189632 | bytes 14712832 | tf_op jit(solution)/shard_map/dot_general | solution.py:47
  773.4 17.8 %convolution_convert_fusion.2 = bf16[2048,2048]{1,0:T(8,128)(2,1)} fusion(bf16[2048,1024]{1,0:T(8,128)(2,1)} %constant_dynamic-update-slice_fusion.1, f32[2048,1024]{1,0:T(8,128)} %copy-done.35, f32[1024]{0:T(1024)S(1)} %copy-done.28), kind=kOutput, calls=%fused_computation.78 | convolution fusion | flops 8615100416 | bytes 20975616 | tf_op jit(solution)/shard_map/dot_general | solution.py:47
  791.2 9.1 convolution_convert_fusion
  801.8 11.3 convert_element_type.149
  828.6 325.0 %all-reduce.13.cloned.1.call-done = (bf16[2048,2048]{1,0:T(8,128)(2,1)}, bf16[2048,2048]{1,0:T(8,128)(2,1)}) async-done(((bf16[2048,2048]{1,0:T(8,128)(2,1)}, bf16[2048,2048]{1,0:T(8,128)(2,1)}), (bf16[2048,2048]{1,0:T(8,128)(2,1)}, bf16[2048,2048]{1,0:T(8,128)(2,1)})) %all-reduce.13.cloned.1.call-update) | async-done | bytes 16777232 | tf_op jit(solution)/shard_map/psum | solution.py:164
  1156.8 5.2 dynamic-slice_reduce_fusion.2
  1165.2 122.8 %all-reduce.11.cloned.1.call-done = (f32[4096]{0:T(1024)}, f32[2048]{0:T(1024)}, f32[8192]{0:T(1024)}, f32[2048]{0:T(1024)}, f32[2048]{0:T(1024)}, /*index=5*/f32[2048]{0:T(1024)}, f32[2048]{0:T(1024)}, f32[2048]{0:T(1024)}) async-done(((f32[4096]{0:T(1024)}, f32[2048]{0:T(1024)}, f32[8192]{0:T(1024)}, f32[2048]{0:T(1024)}, f32[2048]{0:T(1024)}, /*index=5*/f32[2048]{0:T(1024)}, f32[2048]{0:T(1024)}, ...) | async-done | bytes 98320 | tf_op jit(solution)/shard_map/psum | solution.py:295
  (274 shorter events, 194.8 us)
Async XLA Ops:
  7.2 48.4 %all-gather.4.cloned.1.call-start = ((), (), s32[]{:S(2)}) async-start(), calls=%async_computation.4 | async-start | bytes 3932160 | tf_op jit(solution)/shard_map/all_gather | solution.py:75
  9.6 107.9 %all-gather.6.cloned.1.call-start = ((), (), s32[]{:S(2)}) async-start(), calls=%async_computation.5 | async-start | bytes 1310720 | tf_op jit(solution)/shard_map/all_gather | solution.py:76
  11.5 290.1 %all-reduce.7.cloned.1.call-start = ((), (), s32[]{:S(2)}) async-start(), calls=%async_computation.6 | async-start | bytes 16777216 | tf_op jit(solution)/shard_map/psum | solution.py:152
  13.4 42.2 %copy-start.23 = (f32[2048]{0:T(1024)S(1)}, f32[2048]{0:T(1024)}, u32[]{:S(2)}) copy-start(f32[2048]{0:T(1024)} %param.32) | copy-start | bytes 24580
  13.4 42.2 %copy-start.33 = (f32[2048]{0:T(1024)S(1)}, f32[2048]{0:T(1024)}, u32[]{:S(2)}) copy-start(f32[2048]{0:T(1024)} %param.33) | copy-start | bytes 24580
  19.2 282.3 %copy-start.16 = (f32[2048]{0:T(1024)}, f32[2048]{0:T(1024)S(1)}, u32[]{:S(2)}) copy-start(f32[2048]{0:T(1024)S(1)} %broadcast_multiply_fusion.3) | copy-start | bytes 24580
  21.6 280.0 %copy-start.20 = (f32[2048]{0:T(1024)}, f32[2048]{0:T(1024)S(1)}, u32[]{:S(2)}) copy-start(f32[2048]{0:T(1024)S(1)} %add_rsqrt_fusion.1) | copy-start | bytes 24580
  125.8 230.8 %all-gather.8.cloned.1.call-start = ((), (), s32[]{:S(2)}) async-start(), calls=%async_computation.7 | async-start | bytes 5242880 | tf_op jit(solution)/shard_map/all_gather | solution.py:77
  128.4 173.1 %copy-start.26 = (f32[2048]{0:T(1024)S(1)}, f32[2048]{0:T(1024)}, u32[]{:S(2)}) copy-start(f32[2048]{0:T(1024)} %param.27) | copy-start | bytes 24580
  131.4 27.1 %collective-permute-start = (bf16[512,1024]{1,0:T(8,128)(2,1)S(1)}, bf16[512,1024]{1,0:T(8,128)(2,1)}, u32[]{:S(2)}, u32[]{:S(2)}) collective-permute-start(bf16[512,1024]{1,0:T(8,128)(2,1)S(1)} %get-tuple-element.303), channel_id=1, source_target_pairs={{0,8},{8,16},{16,24},{24,0},{1,9},{9,17},{17,25},{25,1},{2,10},{10... | collective-permute-start | bytes 3145736 | tf_op jit(solution)/shard_map/ppermute | solution.py:18
  133.9 446.0 %all-reduce.9.cloned.1.call-start = ((), (), s32[]{:S(2)}) async-start(), calls=%async_computation.8 | async-start | bytes 16777216 | tf_op jit(solution)/shard_map/psum | solution.py:182
  134.0 46.8 %collective-permute-start.1 = (bf16[512,1024]{1,0:T(8,128)(2,1)S(1)}, bf16[512,1024]{1,0:T(8,128)(2,1)S(1)}, u32[]{:S(2)}, u32[]{:S(2)}) collective-permute-start(bf16[512,1024]{1,0:T(8,128)(2,1)S(1)} %get-tuple-element.303), channel_id=1, source_target_pairs={{0,24},{8,0},{16,8},{24,16},{1,25},{9,1},{17,9},{25,17},{2,26},{10... | collective-permute-start | bytes 3145736 | tf_op jit(solution)/shard_map/ppermute | solution.py:23
  158.4 43.7 %collective-permute-start.2 = (bf16[512,1024]{1,0:T(8,128)(2,1)}, bf16[512,1024]{1,0:T(8,128)(2,1)S(1)}, u32[]{:S(2)}, u32[]{:S(2)}) collective-permute-start(bf16[512,1024]{1,0:T(8,128)(2,1)} %collective-permute-done), channel_id=1, source_target_pairs={{0,8},{8,16},{16,24},{24,0},{1,9},{9,17},{17,25},{25,1},{2,10},{10... | collective-permute-start | bytes 3145736 | tf_op jit(solution)/shard_map/ppermute | solution.py:18
  159.6 459.3 %copy-start.27 = (f32[1024]{0:T(1024)}, f32[1024]{0:T(1024)S(1)}, u32[]{:S(2)}) copy-start(f32[1024]{0:T(1024)S(1)} %dynamic_slice.59) | copy-start | bytes 12292
  159.6 459.3 %copy-start.19 = (f32[2048]{0:T(1024)}, f32[2048]{0:T(1024)S(1)}, u32[]{:S(2)}) copy-start(f32[2048]{0:T(1024)S(1)} %compare_convert_fusion) | copy-start | bytes 24580
  326.7 30.0 %copy-start.22 = (f32[2048]{0:T(1024)S(1)}, f32[2048]{0:T(1024)}, u32[]{:S(2)}) copy-start(f32[2048]{0:T(1024)} %param.34) | copy-start | bytes 24580
  326.7 30.0 %copy-start.32 = (f32[2048]{0:T(1024)S(1)}, f32[2048]{0:T(1024)}, u32[]{:S(2)}) copy-start(f32[2048]{0:T(1024)} %param.35) | copy-start | bytes 24580
  369.9 21.4 %copy-start.35 = (f32[2048,1024]{1,0:T(8,128)}, f32[2048,1024]{1,0:T(8,128)S(1)}, u32[]{:S(2)}) copy-start(f32[2048,1024]{1,0:T(8,128)S(1)} %fusion.75) | copy-start | bytes 25165828
  369.9 23.4 %copy-start.30 = (bf16[2048,1024]{1,0:T(8,128)(2,1)S(1)}, bf16[2048,1024]{1,0:T(8,128)(2,1)}, u32[]{:S(2)}) copy-start(bf16[2048,1024]{1,0:T(8,128)(2,1)} %all-gather.8.cloned.1.call-done) | copy-start | bytes 12582916
  404.2 414.6 %reduce-scatter.7.cloned.1.call-start = ((), (), s32[]{:S(2)}) async-start(), calls=%async_computation.10 | async-start | bytes 1310720 | tf_op jit(solution)/shard_map/reduce_scatter | solution.py:285
  590.4 24.8 %copy-start.8 = (bf16[4,512,2,128]{3,2,1,0:T(2,128)(2,1)S(1)}, bf16[4,512,2,128]{3,2,1,0:T(2,128)(2,1)}, u32[]{:S(2)}) copy-start(bf16[4,512,2,128]{3,2,1,0:T(2,128)(2,1)} %get-tuple-element.126) | copy-start | bytes 3145732
  618.8 201.7 %reduce-scatter.11.cloned.1.call-start = ((), (), s32[]{:S(2)}) async-start(), calls=%async_computation.12 | async-start | bytes 5242880 | tf_op jit(solution)/shard_map/reduce_scatter | solution.py:291
  635.8 187.6 %reduce-scatter.9.cloned.1.call-start = ((), (), s32[]{:S(2)}) async-start(), calls=%async_computation.11 | async-start | bytes 5242880 | tf_op jit(solution)/shard_map/reduce_scatter | solution.py:288
  651.2 174.9 %reduce-scatter.5.cloned.1.call-start = ((), (), s32[]{:S(2)}) async-start(), calls=%async_computation.9 | async-start | bytes 3932160 | tf_op jit(solution)/shard_map/reduce_scatter | solution.py:282
  760.2 13.2 %copy-start.28 = (f32[1024]{0:T(1024)S(1)}, f32[1024]{0:T(1024)}, u32[]{:S(2)}) copy-start(f32[1024]{0:T(1024)} %copy-done.27) | copy-start | bytes 12292
  773.3 17.9 %copy-start.9 = (bf16[2048,2,3,128]{0,3,2,1:T(8,128)(2,1)S(1)}, bf16[2048,2,3,128]{0,3,2,1:T(8,128)(2,1)}, u32[]{:S(2)}) copy-start(bf16[2048,2,3,128]{0,3,2,1:T(8,128)(2,1)} %copy.80) | copy-start | bytes 9437188
  773.3 380.3 %all-reduce.13.cloned.1.call-start = ((), (), s32[]{:S(2)}) async-start(), calls=%async_computation.14 | async-start | bytes 33554432 | tf_op jit(solution)/shard_map/psum | solution.py:164
  773.4 17.8 %copy-start.31 = (bf16[2048,768]{1,0:T(8,128)(2,1)S(1)}, bf16[2048,768]{1,0:T(8,128)(2,1)}, u32[]{:S(2)}) copy-start(bf16[2048,768]{1,0:T(8,128)(2,1)} %all-gather.4.cloned.1.call-done) | copy-start | bytes 9437188
  800.4 487.7 %all-reduce.11.cloned.1.call-start = ((), (), s32[]{:S(2)}) async-start(), calls=%async_computation.13 | async-start | bytes 196608 | tf_op jit(solution)/shard_map/psum | solution.py:295
  801.8 11.3 copy-start.15
  818.7 343.3 %copy-start.18 = (f32[16,2,128]{2,1,0:T(2,128)}, f32[16,2,128]{2,1,0:T(2,128)S(1)}, u32[]{:S(2)}) copy-start(f32[16,2,128]{2,1,0:T(2,128)S(1)} %constant_dynamic-update-slice_fusion) | copy-start | bytes 49156
  823.3 338.7 %copy-start.25 = (f32[2048]{0:T(1024)S(1)}, f32[2048]{0:T(1024)}, u32[]{:S(2)}) copy-start(f32[2048]{0:T(1024)} %param.31) | copy-start | bytes 24580
  (31 other events, 162.4 us)
Sparse Core Ops, SparseCore 0:
  10.4 45.1 all-gather.3
  58.0 26.6 all-gather.5
  125.9 175.5 all-reduce.6
  303.8 52.8 all-gather.7
  404.3 175.5 all-reduce.8
  619.0 27.8 reduce-scatter.6
  650.1 52.6 reduce-scatter.10
  705.8 52.6 reduce-scatter.8
  773.5 43.8 reduce-scatter.4
  820.0 333.5 all-reduce.12
  1162.3 125.6 all-reduce.10
